TPU v7x, 512 devices: a whole 4x4x16 slice. The times are simulated.
512 devices in a mesh: section: 16 (over z), batch: 32 (over x, y, core).
Axes of the slice: x: 4, y: 4, z: 16, core: 2. Of those that a mesh axis runs over, the one named last changes fastest.
Arguments:
- images: bfloat16 [32, 256, 1536], P('batch'), may hold values from -10 to 10
- weights: bfloat16 [16, 6, 256, 256], P('section'), may hold values from -0.375 to 0.375
- bn_mean: float32 [16, 1536], P('section'), may hold values from -3 to 3
- bn_var: float32 [16, 1536], P('section'), may hold values from 0.25 to 2
- bn_gain: float32 [16, 1536], P('section'), may hold values from 0.1 to 1.9
- bn_bias: float32 [16, 1536], P('section'), may hold values from -3 to 3
Outputs:
- image_grad: bfloat16 [32, 256, 1536], P('batch', 'section')
- loss_value: float32 [], replicated
All inputs are finite; a program needn't handle non-finite values.
Results may differ from a plain program's by a relative error of at most 0.013.
Values may be sent and summed in bfloat16 or wider, within the bound.
No kernel may reach another device: no remote copies, remote signals or barrier semaphores. Data moves between devices by JAX's collectives and lax.ppermute only.
A program may use at most 64 MiB of HBM per device.

v0:
```python
import jax
import jax.numpy as jnp
from jax import lax
from jax.sharding import PartitionSpec as P

BLOCK = 512
MICRO = 8
EPS = 1e-05
HIGHEST = lax.Precision.HIGHEST


def from_behind(value, axis, steps):
    count = lax.axis_size(axis)
    first, last = (max(0, -steps), min(count, count - steps))
    return lax.ppermute(value, axis, [(source, source + steps) for source in range(first, last)])


def group_forward(hidden, weight):
    row_total = hidden.shape[0]
    groups, in_width, out_width = weight.shape
    pieces = hidden.reshape(row_total, groups, in_width)
    result = jnp.einsum("rgi,gio->rgo", pieces, weight, preferred_element_type=jnp.float32)
    return result.reshape(row_total, groups * out_width)


def group_backward(upstream, weight):
    row_total = upstream.shape[0]
    groups, in_width, out_width = weight.shape
    pieces = upstream.reshape(row_total, groups, out_width)
    result = jnp.einsum("rgo,gio->rgi", pieces, weight, preferred_element_type=jnp.float32)
    return result.reshape(row_total, groups * in_width)


def block_gram(pre_act, center, block_width):
    row_total, channels = pre_act.shape
    centered = (pre_act - center).reshape(row_total, channels // block_width, block_width)
    return jnp.einsum("rbi,rbj->bij", centered, centered, precision=HIGHEST)


def shards(images, weights, bn_mean, bn_var, bn_gain, bn_bias):
    sections = lax.axis_size("section")
    position = lax.axis_index("section")
    group_rows = images.shape[1]
    channels = images.shape[2]
    micro_rows = group_rows // MICRO
    block_count = channels // BLOCK
    row_total = group_rows * lax.axis_size("batch")
    weight = weights[0]
    run_mean = bn_mean[0]
    run_var = bn_var[0]
    bn_scale = bn_gain[0] * lax.rsqrt(run_var + EPS)
    bn_shift = bn_bias[0]
    source = images[0].reshape(MICRO, micro_rows, channels)
    tick_count = MICRO + sections - 1
    gram_shape = (1, 1, 1)
    stored_type = jnp.float32

    def forward_tick(tick_index, loop_vars):
        incoming, stored, sum_pre, sum_gram = loop_vars
        offset_raw = tick_index - position
        in_range = (offset_raw >= 0) & (offset_raw < MICRO)
        slot_index = jnp.clip(offset_raw, 0, MICRO - 1)
        entering = lax.dynamic_index_in_dim(source, slot_index, 0, keepdims=False)
        hidden = jnp.where(position == 0, entering, incoming)

        def forward_active_step(hidden_in):
            pre_act = group_forward(hidden_in, weight)
            emitted = jax.nn.silu((pre_act - run_mean) * bn_scale + bn_shift).astype(jnp.bfloat16)
            block_sums = jnp.zeros(gram_shape, jnp.float32)
            return (pre_act, emitted, jnp.sum(pre_act, axis=0), block_sums)

        def forward_bubble_step(hidden_in):
            return (
                jnp.zeros((micro_rows, channels), jnp.float32),
                jnp.zeros((micro_rows, channels), jnp.bfloat16),
                jnp.zeros((channels,), jnp.float32),
                jnp.zeros(gram_shape, jnp.float32),
            )

        pre_act, emitted, part_sum, block_sums = lax.cond(
            in_range, forward_active_step, forward_bubble_step, hidden
        )
        previous = lax.dynamic_index_in_dim(stored, slot_index, 0, keepdims=False)
        stored = lax.dynamic_update_index_in_dim(
            stored, jnp.where(in_range, pre_act, previous), slot_index, 0
        )
        incoming = from_behind(emitted, "section", 1)
        return (incoming, stored, sum_pre + part_sum, sum_gram + block_sums)

    start_vars = (
        jnp.zeros((micro_rows, channels), jnp.bfloat16),
        jnp.zeros((MICRO, micro_rows, channels), stored_type),
        jnp.zeros((channels,), jnp.float32),
        jnp.zeros(gram_shape, jnp.float32),
    )
    incoming, stored, sum_pre, sum_gram = lax.fori_loop(0, tick_count, forward_tick, start_vars)
    total_sum = lax.psum(sum_pre, "batch")
    batch_mean = total_sum / row_total
    flat_saved = stored.reshape(group_rows, channels)
    covariance = lax.psum(block_gram(flat_saved, batch_mean, BLOCK), "batch") / row_total
    var_blocks = run_var.reshape(block_count, BLOCK)
    deviation = covariance - var_blocks[:, :, None] * jnp.eye(BLOCK, dtype=jnp.float32)[None]
    layer_term = jnp.sum((batch_mean - run_mean) ** 2) + 0.25 * jnp.sum(deviation**2)
    loss_value = lax.psum(layer_term, "section") / (sections * channels)
    mean_pull = 2.0 * (batch_mean - run_mean)

    def backward_tick(tick_index, loop_vars):
        incoming, image_grads = loop_vars
        offset_raw = tick_index - (sections - 1 - position)
        in_range = (offset_raw >= 0) & (offset_raw < MICRO)
        slot_index = jnp.clip(offset_raw, 0, MICRO - 1)
        stored_item = lax.dynamic_index_in_dim(stored, slot_index, 0, keepdims=False)

        def backward_active_step(operands):
            item_in, upstream = operands
            active = (item_in - run_mean) * bn_scale + bn_shift
            sig_value = jax.nn.sigmoid(active)
            silu_slope = sig_value * (1.0 + active * (1.0 - sig_value))
            centered = (item_in - batch_mean).reshape(micro_rows, block_count, BLOCK)
            cov_pull = jnp.einsum("rbi,bij->rbj", centered, deviation, precision=HIGHEST).reshape(
                micro_rows, channels
            )
            pre_grad = (
                upstream.astype(jnp.float32) * silu_slope * bn_scale + mean_pull + cov_pull
            ).astype(jnp.bfloat16)
            return group_backward(pre_grad, weight).astype(jnp.bfloat16)

        def backward_bubble_step(operands):
            return jnp.zeros((micro_rows, channels), jnp.bfloat16)

        sent_back = lax.cond(
            in_range, backward_active_step, backward_bubble_step, (stored_item, incoming)
        )
        previous = lax.dynamic_index_in_dim(image_grads, slot_index, 0, keepdims=False)
        image_grads = lax.dynamic_update_index_in_dim(
            image_grads, jnp.where(in_range, sent_back, previous), slot_index, 0
        )
        incoming = from_behind(sent_back, "section", -1)
        return (incoming, image_grads)

    back_vars = (
        jnp.zeros((micro_rows, channels), jnp.bfloat16),
        jnp.zeros((MICRO, micro_rows, channels), jnp.bfloat16),
    )
    incoming, image_grads = lax.fori_loop(0, tick_count, backward_tick, back_vars)
    flat_grads = image_grads.reshape(group_rows, channels)
    own_term = jnp.where(
        position == 0,
        flat_grads.astype(jnp.float32),
        jnp.zeros((group_rows, channels), jnp.float32),
    )
    own_rows = lax.psum_scatter(
        own_term.astype(jnp.bfloat16), "section", scatter_dimension=0, tiled=True
    )
    return (own_rows[None], loss_value)


def solution(mesh):
    placed = (
        P("batch", None, None),
        P("section", None, None, None),
        P("section", None),
        P("section", None),
        P("section", None),
        P("section", None),
    )
    return jax.shard_map(
        shards,
        mesh=mesh,
        in_specs=placed,
        out_specs=(P("batch", "section", None), P()),
        check_vma=False,
    )
```

profile of v0, /device:TPU:8, one launch (start us, length us, event | category | flops | bytes accessed | tf_op | source)
XLA Modules:
  0.0 880.5 jit_solution(1067873683740494981)
XLA Ops:
  8.2 234.9 %while.37 = (s32[]{:T(128)}, bf16[32,1536]{1,0:T(8,128)(2,1)S(1)}, f32[8,32,1536]{2,1,0:T(8,128)S(1)}, f32[1536]{0:T(1024)S(1)}, s32[]{:T(128)}, /*index=5*/pred...) while((s32[]{:T(128)}, bf16[32,1536]{1,0:T(8,128)(2,1)S(1)}, ...), condition=%wide.region_4.5_spmd.clone, body=%wide.region_0.4_spmd.clone.sunk | while | flops 25708040 | bytes 3520875 | solution.py:96
  8.2 5.4 conditional.6
  17.3 5.4 conditional.6
  29.3 5.4 conditional.6
  41.2 5.4 conditional.6
  53.2 5.4 conditional.6
  65.1 5.4 conditional.6
  77.1 5.4 conditional.6
  89.0 5.4 conditional.6
  101.6 9.0 %collective-permute-start.1 = (bf16[32,1536]{1,0:T(8,128)(2,1)S(1)}, bf16[32,1536]{1,0:T(8,128)(2,1)S(1)}, u32[]{:S(2)}, u32[]{:S(2)}) collective-permute-start(bf16[32,1536]{1,0:T(8,128)(2,1)S(1)} %get-tuple-element.842), channel_id=1, source_target_pairs={{0,32},{32,64},{64,96},{96,128},{128,160},{160,192},{192,224},{224... | collective-permute-start | bytes 294920 | tf_op jit(solution)/shard_map/while/body/eval_jaxpr/ppermute | solution.py:15
  121.1 6.4 collective-permute-start.1
  130.4 5.5 collective-permute-start.1
  139.3 9.8 %collective-permute-start.1 = (bf16[32,1536]{1,0:T(8,128)(2,1)S(1)}, bf16[32,1536]{1,0:T(8,128)(2,1)S(1)}, u32[]{:S(2)}, u32[]{:S(2)}) collective-permute-start(bf16[32,1536]{1,0:T(8,128)(2,1)S(1)} %get-tuple-element.842), channel_id=1, source_target_pairs={{0,32},{32,64},{64,96},{96,128},{128,160},{160,192},{192,224},{224... | collective-permute-start | bytes 294920 | tf_op jit(solution)/shard_map/while/body/eval_jaxpr/ppermute | solution.py:15
  152.0 6.7 collective-permute-start.1
  161.6 9.6 %collective-permute-start.1 = (bf16[32,1536]{1,0:T(8,128)(2,1)S(1)}, bf16[32,1536]{1,0:T(8,128)(2,1)S(1)}, u32[]{:S(2)}, u32[]{:S(2)}) collective-permute-start(bf16[32,1536]{1,0:T(8,128)(2,1)S(1)} %get-tuple-element.842), channel_id=1, source_target_pairs={{0,32},{32,64},{64,96},{96,128},{128,160},{160,192},{192,224},{224... | collective-permute-start | bytes 294920 | tf_op jit(solution)/shard_map/while/body/eval_jaxpr/ppermute | solution.py:15
  175.0 5.5 collective-permute-start.1
  183.4 5.5 collective-permute-start.1
  191.8 5.5 collective-permute-start.1
  200.3 5.9 collective-permute-start.1
  209.1 5.6 collective-permute-start.1
  217.6 5.6 collective-permute-start.1
  226.1 5.5 collective-permute-start.1
  234.6 6.4 collective-permute-start.1
  243.1 64.5 %psum.21 = f32[1536]{0:T(1024)S(1)} all-reduce(f32[1536]{0:T(1024)S(1)} %get-tuple-element.603), channel_id=1, replica_groups=mesh['section'=16,'batch'=32] {'batch'}, use_global_device_ids=true, to_apply=%region_5.6 | all-reduce | flops 1536 | bytes 12288 | tf_op jit(solution)/shard_map/psum | solution.py:97
  313.2 5.1 fusion.9
  319.6 166.5 %all-reduce.2.cloned.1.call-done = f32[3,512,512]{2,1,0:T(8,128)} async-done(((f32[3,512,512]{2,1,0:T(8,128)}), f32[3,512,512]{2,1,0:T(8,128)}) %all-reduce.2.cloned.1.call-update) | async-done | bytes 3145744 | tf_op jit(solution)/shard_map/psum | solution.py:100
  490.9 318.2 %while.36 = (s32[]{:T(128)}, bf16[32,1536]{1,0:T(8,128)(2,1)S(1)}, bf16[8,32,1536]{2,1,0:T(8,128)(2,1)}, s32[]{:T(128)}, f32[8,32,1536]{2,1,0:T(8,128)}, /*index...) while((s32[]{:T(128)}, bf16[32,1536]{1,0:T(8,128)(2,1)S(1)}, ...), condition=%wide.region_10.11_spmd, body=%wide.region_7.10_spmd.sunk | while | flops 328089600 | bytes 7834472 | solution.py:145
  527.7 4.9 collective-permute-done
  535.5 6.1 collective-permute-done
  544.5 5.0 collective-permute-done
  567.5 4.9 collective-permute-done
  582.9 4.9 collective-permute-done
  598.4 89.0 %collective-permute-done = bf16[32,1536]{1,0:T(8,128)(2,1)S(1)} collective-permute-done((bf16[32,1536]{1,0:T(8,128)(2,1)S(1)}, bf16[32,1536]{1,0:T(8,128)(2,1)S(1)}, u32[]{:S(2)}, u32[]{:S(2)}) %collective-permute-start) | collective-permute-done | bytes 98336 | tf_op jit(solution)/shard_map/while/body/eval_jaxpr/ppermute | solution.py:15
  687.4 7.3 conditional.5
  697.6 5.6 collective-permute-done
  703.3 7.3 conditional.5
  713.4 5.7 collective-permute-done
  719.2 7.3 conditional.5
  733.9 7.3 conditional.5
  748.8 7.3 conditional.5
  759.0 5.3 collective-permute-done
  764.3 7.3 conditional.5
  774.4 4.9 collective-permute-done
  779.3 7.3 conditional.5
  789.5 5.8 collective-permute-done
  795.3 7.3 conditional.5
  812.5 27.6 %psum.23 = f32[]{:T(128)} all-reduce(f32[]{:T(128)S(6)} %add.132), channel_id=1, replica_groups=mesh['section'=16,'batch'=32] {'section'}, use_global_device_ids=true, to_apply=%region_14.15 | all-reduce | flops 1 | bytes 8 | tf_op jit(solution)/shard_map/psum | solution.py:104
  840.7 31.7 %reduce-scatter.2.cloned.1.call-done = bf16[16,1536]{1,0:T(8,128)(2,1)} async-done(((bf16[256,1536]{1,0:T(8,128)(2,1)}), bf16[16,1536]{1,0:T(8,128)(2,1)}) %reduce-scatter.2.cloned.1.call-update) | async-done | bytes 49168 | tf_op jit(solution)/shard_map/reduce_scatter | solution.py:152
  (441 shorter events, 341.9 us)
Async XLA Ops:
  7.2 479.0 %all-reduce.2.cloned.1.call-start = ((), (), s32[]{:S(2)}) async-start(), calls=%async_computation.1 | async-start | bytes 6291456 | tf_op jit(solution)/shard_map/psum | solution.py:100
  13.7 3.6 collective-permute-start.1
  22.7 6.6 collective-permute-start.1
  34.7 6.5 collective-permute-start.1
  46.7 6.5 collective-permute-start.1
  58.6 6.5 collective-permute-start.1
  70.5 6.5 collective-permute-start.1
  82.5 6.5 collective-permute-start.1
  94.4 6.5 collective-permute-start.1
  101.6 11.2 %collective-permute-start.1 = (bf16[32,1536]{1,0:T(8,128)(2,1)S(1)}, bf16[32,1536]{1,0:T(8,128)(2,1)S(1)}, u32[]{:S(2)}, u32[]{:S(2)}) collective-permute-start(bf16[32,1536]{1,0:T(8,128)(2,1)S(1)} %get-tuple-element.842), channel_id=1, source_target_pairs={{0,32},{32,64},{64,96},{96,128},{128,160},{160,192},{192,224},{224... | collective-permute-start | bytes 294920 | tf_op jit(solution)/shard_map/while/body/eval_jaxpr/ppermute | solution.py:15
  113.6 6.8 collective-permute-start.1
  121.1 8.6 collective-permute-start.1
  130.4 8.2 collective-permute-start.1
  139.3 12.0 %collective-permute-start.1 = (bf16[32,1536]{1,0:T(8,128)(2,1)S(1)}, bf16[32,1536]{1,0:T(8,128)(2,1)S(1)}, u32[]{:S(2)}, u32[]{:S(2)}) collective-permute-start(bf16[32,1536]{1,0:T(8,128)(2,1)S(1)} %get-tuple-element.842), channel_id=1, source_target_pairs={{0,32},{32,64},{64,96},{96,128},{128,160},{160,192},{192,224},{224... | collective-permute-start | bytes 294920 | tf_op jit(solution)/shard_map/while/body/eval_jaxpr/ppermute | solution.py:15
  152.0 8.9 %collective-permute-start.1 = (bf16[32,1536]{1,0:T(8,128)(2,1)S(1)}, bf16[32,1536]{1,0:T(8,128)(2,1)S(1)}, u32[]{:S(2)}, u32[]{:S(2)}) collective-permute-start(bf16[32,1536]{1,0:T(8,128)(2,1)S(1)} %get-tuple-element.842), channel_id=1, source_target_pairs={{0,32},{32,64},{64,96},{96,128},{128,160},{160,192},{192,224},{224... | collective-permute-start | bytes 294920 | tf_op jit(solution)/shard_map/while/body/eval_jaxpr/ppermute | solution.py:15
  161.6 12.6 %collective-permute-start.1 = (bf16[32,1536]{1,0:T(8,128)(2,1)S(1)}, bf16[32,1536]{1,0:T(8,128)(2,1)S(1)}, u32[]{:S(2)}, u32[]{:S(2)}) collective-permute-start(bf16[32,1536]{1,0:T(8,128)(2,1)S(1)} %get-tuple-element.842), channel_id=1, source_target_pairs={{0,32},{32,64},{64,96},{96,128},{128,160},{160,192},{192,224},{224... | collective-permute-start | bytes 294920 | tf_op jit(solution)/shard_map/while/body/eval_jaxpr/ppermute | solution.py:15
  175.0 7.7 collective-permute-start.1
  183.4 7.7 collective-permute-start.1
  191.8 7.7 collective-permute-start.1
  200.3 8.1 collective-permute-start.1
  209.1 7.8 collective-permute-start.1
  217.6 7.8 collective-permute-start.1
  226.1 7.7 collective-permute-start.1
  234.6 8.6 collective-permute-start.1
  318.4 554.1 %reduce-scatter.2.cloned.1.call-start = ((), (), s32[]{:S(2)}) async-start(), calls=%async_computation.2 | async-start | bytes 835584 | tf_op jit(solution)/shard_map/reduce_scatter | solution.py:152
  491.0 6.7 collective-permute-start
  497.7 6.5 collective-permute-start
  504.2 6.5 collective-permute-start
  510.8 6.5 collective-permute-start
  517.3 7.6 collective-permute-start
  524.9 7.7 collective-permute-start
  532.6 9.0 %collective-permute-start = (bf16[32,1536]{1,0:T(8,128)(2,1)S(1)}, bf16[32,1536]{1,0:T(8,128)(2,1)S(1)}, u32[]{:S(2)}, u32[]{:S(2)}) collective-permute-start(bf16[32,1536]{1,0:T(8,128)(2,1)S(1)} %get-tuple-element.944), channel_id=1, source_target_pairs={{32,0},{64,32},{96,64},{128,96},{160,128},{192,160},{224,192},{256... | collective-permute-start | bytes 294920 | tf_op jit(solution)/shard_map/while/body/eval_jaxpr/ppermute | solution.py:15
  541.6 7.9 collective-permute-start
  549.5 7.6 collective-permute-start
  557.1 7.4 collective-permute-start
  564.6 7.7 collective-permute-start
  572.3 7.7 collective-permute-start
  580.1 7.7 collective-permute-start
  587.8 7.7 collective-permute-start
  595.6 91.9 %collective-permute-start = (bf16[32,1536]{1,0:T(8,128)(2,1)S(1)}, bf16[32,1536]{1,0:T(8,128)(2,1)S(1)}, u32[]{:S(2)}, u32[]{:S(2)}) collective-permute-start(bf16[32,1536]{1,0:T(8,128)(2,1)S(1)} %get-tuple-element.944), channel_id=1, source_target_pairs={{32,0},{64,32},{96,64},{128,96},{160,128},{192,160},{224,192},{256... | collective-permute-start | bytes 294920 | tf_op jit(solution)/shard_map/while/body/eval_jaxpr/ppermute | solution.py:15
  694.7 8.5 collective-permute-start
  710.6 8.6 collective-permute-start
  726.5 7.5 collective-permute-start
  741.2 7.5 collective-permute-start
  756.1 8.2 collective-permute-start
  771.6 7.7 collective-permute-start
  786.6 8.7 collective-permute-start
  802.6 6.6 collective-permute-start
  (3 other events, 412.7 us)
Sparse Core Ops, SparseCore 0:
  318.5 167.5 all-reduce.1
  811.4 61.0 reduce-scatter.1
where the time goes:
time: 885 us; the launch traced here: 880 us
  waiting for transfers between devices  434 us (49%)
  starting transfers between devices  158 us (18%)
  blocking collectives  92.1 us (10%)
  other arithmetic  70.8 us (8%)
  local copies, waits for them, and re-layouts  62.6 us (7%)
  matrix products  43.3 us (5%)
  between operations  17.1 us (2%)
    ppermute x46, waiting for transfers between devices, from_behind(): lax.ppermute(value, axis, [(source, source + steps) for source in range(f...  236 us
    psum x1, waiting for transfers between devices, shards(): lax.psum(block_gram(flat_saved, batch_mean, BLOCK), 'batch') / row_total  166 us
    ppermute x46, starting transfers between devices, from_behind(): lax.ppermute(value, axis, [(source, source + steps) for source in range(f...  158 us
    psum x1, blocking collectives, shards(): total_sum = lax.psum(sum_pre, 'batch')  64.5 us
    reduce_scatter x1, waiting for transfers between devices, shards(): lax.psum_scatter(own_term.astype(jnp.bfloat16), 'section', scatter_dimens...  31.7 us
    psum x1, blocking collectives, shards(): loss_value = lax.psum(layer_term, 'section') / (sections * channels)  27.6 us
    dynamic_slice x23, local copies, waits for them, and re-layouts, backward_tick(): lax.dynamic_index_in_dim(image_grads, slot_index, 0, keepdims=False)  20.8 us
  transfers between devices with their start and end apart: 48, of which 48 were waited for; matrix products, arithmetic and copies ran while one was open for 5% of the time, Pallas kernels for 0%

commit v1 on v0

--- a/solution.py
+++ b/solution.py
@@ -94,7 +94,8 @@
         jnp.zeros(gram_shape, jnp.float32),
     )
     incoming, stored, sum_pre, sum_gram = lax.fori_loop(0, tick_count, forward_tick, start_vars)
-    total_sum = lax.psum(sum_pre, "batch")
+    shards_2 = lax.all_gather(sum_pre, "batch")
+    total_sum = jnp.sum(shards_2, axis=0)
     batch_mean = total_sum / row_total
     flat_saved = stored.reshape(group_rows, channels)
     covariance = lax.psum(block_gram(flat_saved, batch_mean, BLOCK), "batch") / row_total

time: 885 us -> 847 us (0.957)
  blocking collectives: 92.1 us -> 55.8 us
    psum x1 -> x0, blocking collectives: 64.5 us -> none  [shards(): total_sum = lax.psum(sum_pre, 'batch')]
    all_gather x0 -> x1, blocking collectives: none -> 28.2 us  [shards(): shards_2 = lax.all_gather(sum_pre, 'batch')]
  transfers between devices with their start and end apart: 48 -> 48, of which waited for: 48 -> 48; matrix products, arithmetic and copies ran while one was open for 5% -> 6% of each run, Pallas kernels for 0% -> 0%
where the time goes in v1:
time: 847 us; the launch traced here: 842 us
  waiting for transfers between devices  432 us (51%)
  starting transfers between devices  158 us (19%)
  other arithmetic  70.9 us (8%)
  local copies, waits for them, and re-layouts  62.6 us (7%)
  blocking collectives  55.8 us (7%)
  matrix products  43.3 us (5%)
  between operations  17.1 us (2%)
    ppermute x46, waiting for transfers between devices, from_behind(): lax.ppermute(value, axis, [(source, source + steps) for source in range(f...  236 us
    psum x1, waiting for transfers between devices, shards(): lax.psum(block_gram(flat_saved, batch_mean, BLOCK), 'batch') / row_total  164 us
    ppermute x46, starting transfers between devices, from_behind(): lax.ppermute(value, axis, [(source, source + steps) for source in range(f...  158 us
    reduce_scatter x1, waiting for transfers between devices, shards(): lax.psum_scatter(own_term.astype(jnp.bfloat16), 'section', scatter_dimens...  31.7 us
    all_gather x1, blocking collectives, shards(): shards_2 = lax.all_gather(sum_pre, 'batch')  28.2 us
    psum x1, blocking collectives, shards(): loss_value = lax.psum(layer_term, 'section') / (sections * channels)  27.6 us
    dynamic_slice x23, local copies, waits for them, and re-layouts, backward_tick(): lax.dynamic_index_in_dim(image_grads, slot_index, 0, keepdims=False)  20.8 us
  transfers between devices with their start and end apart: 48, of which 48 were waited for; matrix products, arithmetic and copies ran while one was open for 6% of the time, Pallas kernels for 0%

profile of v1, /device:TPU:8, one launch (start us, length us, event | category | flops | bytes accessed | tf_op | source)
XLA Modules:
  0.0 842.2 jit_solution(1508336327803027534)
XLA Ops:
  8.2 234.9 %while.37 = (s32[]{:T(128)}, bf16[32,1536]{1,0:T(8,128)(2,1)S(1)}, f32[8,32,1536]{2,1,0:T(8,128)S(1)}, f32[1536]{0:T(1024)S(1)}, s32[]{:T(128)}, /*index=5*/pred...) while((s32[]{:T(128)}, bf16[32,1536]{1,0:T(8,128)(2,1)S(1)}, ...), condition=%wide.region_4.5_spmd.clone, body=%wide.region_0.4_spmd.clone.sunk | while | flops 25708040 | bytes 3520875 | solution.py:96
  8.2 5.4 conditional.6
  17.3 5.4 conditional.6
  29.3 5.4 conditional.6
  41.2 5.4 conditional.6
  53.2 5.4 conditional.6
  65.1 5.4 conditional.6
  77.1 5.4 conditional.6
  89.0 5.4 conditional.6
  101.6 9.0 %collective-permute-start.1 = (bf16[32,1536]{1,0:T(8,128)(2,1)S(1)}, bf16[32,1536]{1,0:T(8,128)(2,1)S(1)}, u32[]{:S(2)}, u32[]{:S(2)}) collective-permute-start(bf16[32,1536]{1,0:T(8,128)(2,1)S(1)} %get-tuple-element.842), channel_id=1, source_target_pairs={{0,32},{32,64},{64,96},{96,128},{128,160},{160,192},{192,224},{224... | collective-permute-start | bytes 294920 | tf_op jit(solution)/shard_map/while/body/eval_jaxpr/ppermute | solution.py:15
  121.1 6.4 collective-permute-start.1
  130.4 5.5 collective-permute-start.1
  139.3 9.8 %collective-permute-start.1 = (bf16[32,1536]{1,0:T(8,128)(2,1)S(1)}, bf16[32,1536]{1,0:T(8,128)(2,1)S(1)}, u32[]{:S(2)}, u32[]{:S(2)}) collective-permute-start(bf16[32,1536]{1,0:T(8,128)(2,1)S(1)} %get-tuple-element.842), channel_id=1, source_target_pairs={{0,32},{32,64},{64,96},{96,128},{128,160},{160,192},{192,224},{224... | collective-permute-start | bytes 294920 | tf_op jit(solution)/shard_map/while/body/eval_jaxpr/ppermute | solution.py:15
  152.0 6.7 collective-permute-start.1
  161.6 9.6 %collective-permute-start.1 = (bf16[32,1536]{1,0:T(8,128)(2,1)S(1)}, bf16[32,1536]{1,0:T(8,128)(2,1)S(1)}, u32[]{:S(2)}, u32[]{:S(2)}) collective-permute-start(bf16[32,1536]{1,0:T(8,128)(2,1)S(1)} %get-tuple-element.842), channel_id=1, source_target_pairs={{0,32},{32,64},{64,96},{96,128},{128,160},{160,192},{192,224},{224... | collective-permute-start | bytes 294920 | tf_op jit(solution)/shard_map/while/body/eval_jaxpr/ppermute | solution.py:15
  175.0 5.5 collective-permute-start.1
  183.4 5.5 collective-permute-start.1
  191.8 5.5 collective-permute-start.1
  200.3 5.9 collective-permute-start.1
  209.1 5.6 collective-permute-start.1
  217.6 5.6 collective-permute-start.1
  226.1 5.5 collective-permute-start.1
  234.6 6.4 collective-permute-start.1
  243.1 28.2 %all-gather.1 = f32[32,1,1536]{2,1,0:T(1,128)S(1)} all-gather(f32[1,1,1536]{2,1,0:T(1,128)S(1)} %reshape.74), channel_id=2, replica_groups=mesh['section'=16,'batch'=32] {'batch'}, dimensions={0}, use_global_device_ids=true | all-gather | bytes 202752 | tf_op jit(solution)/shard_map/all_gather | solution.py:97
  277.0 5.1 fusion.9
  283.4 164.5 %all-reduce.2.cloned.1.call-done = f32[3,512,512]{2,1,0:T(8,128)} async-done(((f32[3,512,512]{2,1,0:T(8,128)}), f32[3,512,512]{2,1,0:T(8,128)}) %all-reduce.2.cloned.1.call-update) | async-done | bytes 3145744 | tf_op jit(solution)/shard_map/psum | solution.py:101
  452.7 318.2 %while.36 = (s32[]{:T(128)}, bf16[32,1536]{1,0:T(8,128)(2,1)S(1)}, bf16[8,32,1536]{2,1,0:T(8,128)(2,1)}, s32[]{:T(128)}, f32[8,32,1536]{2,1,0:T(8,128)}, /*index...) while((s32[]{:T(128)}, bf16[32,1536]{1,0:T(8,128)(2,1)S(1)}, ...), condition=%wide.region_10.11_spmd, body=%wide.region_7.10_spmd.sunk | while | flops 328089600 | bytes 7834472 | solution.py:146
  489.5 4.9 collective-permute-done
  497.2 6.1 collective-permute-done
  506.2 5.0 collective-permute-done
  537.0 4.9 collective-permute-done
  552.4 4.9 collective-permute-done
  560.2 89.0 %collective-permute-done = bf16[32,1536]{1,0:T(8,128)(2,1)S(1)} collective-permute-done((bf16[32,1536]{1,0:T(8,128)(2,1)S(1)}, bf16[32,1536]{1,0:T(8,128)(2,1)S(1)}, u32[]{:S(2)}, u32[]{:S(2)}) %collective-permute-start) | collective-permute-done | bytes 98336 | tf_op jit(solution)/shard_map/while/body/eval_jaxpr/ppermute | solution.py:15
  649.2 7.3 conditional.5
  659.4 5.6 collective-permute-done
  665.0 7.3 conditional.5
  675.2 5.7 collective-permute-done
  680.9 7.3 conditional.5
  695.7 7.3 conditional.5
  710.5 7.3 conditional.5
  720.7 5.3 collective-permute-done
  726.0 7.3 conditional.5
  736.2 4.9 collective-permute-done
  741.1 7.3 conditional.5
  751.2 5.8 collective-permute-done
  757.0 7.3 conditional.5
  774.2 27.6 %psum.15 = f32[]{:T(128)} all-reduce(f32[]{:T(128)S(6)} %add.130), channel_id=1, replica_groups=mesh['section'=16,'batch'=32] {'section'}, use_global_device_ids=true, to_apply=%region_14.15 | all-reduce | flops 1 | bytes 8 | tf_op jit(solution)/shard_map/psum | solution.py:105
  802.5 31.7 %reduce-scatter.2.cloned.1.call-done = bf16[16,1536]{1,0:T(8,128)(2,1)} async-done(((bf16[256,1536]{1,0:T(8,128)(2,1)}), bf16[16,1536]{1,0:T(8,128)(2,1)}) %reduce-scatter.2.cloned.1.call-update) | async-done | bytes 49168 | tf_op jit(solution)/shard_map/reduce_scatter | solution.py:153
  (443 shorter events, 342.0 us)
Async XLA Ops:
  7.2 440.7 %all-reduce.2.cloned.1.call-start = ((), (), s32[]{:S(2)}) async-start(), calls=%async_computation.1 | async-start | bytes 6291456 | tf_op jit(solution)/shard_map/psum | solution.py:101
  13.7 3.6 collective-permute-start.1
  22.7 6.6 collective-permute-start.1
  34.7 6.5 collective-permute-start.1
  46.7 6.5 collective-permute-start.1
  58.6 6.5 collective-permute-start.1
  70.5 6.5 collective-permute-start.1
  82.5 6.5 collective-permute-start.1
  94.4 6.5 collective-permute-start.1
  101.6 11.2 %collective-permute-start.1 = (bf16[32,1536]{1,0:T(8,128)(2,1)S(1)}, bf16[32,1536]{1,0:T(8,128)(2,1)S(1)}, u32[]{:S(2)}, u32[]{:S(2)}) collective-permute-start(bf16[32,1536]{1,0:T(8,128)(2,1)S(1)} %get-tuple-element.842), channel_id=1, source_target_pairs={{0,32},{32,64},{64,96},{96,128},{128,160},{160,192},{192,224},{224... | collective-permute-start | bytes 294920 | tf_op jit(solution)/shard_map/while/body/eval_jaxpr/ppermute | solution.py:15
  113.6 6.8 collective-permute-start.1
  121.1 8.6 %collective-permute-start.1 = (bf16[32,1536]{1,0:T(8,128)(2,1)S(1)}, bf16[32,1536]{1,0:T(8,128)(2,1)S(1)}, u32[]{:S(2)}, u32[]{:S(2)}) collective-permute-start(bf16[32,1536]{1,0:T(8,128)(2,1)S(1)} %get-tuple-element.842), channel_id=1, source_target_pairs={{0,32},{32,64},{64,96},{96,128},{128,160},{160,192},{192,224},{224... | collective-permute-start | bytes 294920 | tf_op jit(solution)/shard_map/while/body/eval_jaxpr/ppermute | solution.py:15
  130.4 8.2 collective-permute-start.1
  139.3 12.0 %collective-permute-start.1 = (bf16[32,1536]{1,0:T(8,128)(2,1)S(1)}, bf16[32,1536]{1,0:T(8,128)(2,1)S(1)}, u32[]{:S(2)}, u32[]{:S(2)}) collective-permute-start(bf16[32,1536]{1,0:T(8,128)(2,1)S(1)} %get-tuple-element.842), channel_id=1, source_target_pairs={{0,32},{32,64},{64,96},{96,128},{128,160},{160,192},{192,224},{224... | collective-permute-start | bytes 294920 | tf_op jit(solution)/shard_map/while/body/eval_jaxpr/ppermute | solution.py:15
  152.0 8.9 %collective-permute-start.1 = (bf16[32,1536]{1,0:T(8,128)(2,1)S(1)}, bf16[32,1536]{1,0:T(8,128)(2,1)S(1)}, u32[]{:S(2)}, u32[]{:S(2)}) collective-permute-start(bf16[32,1536]{1,0:T(8,128)(2,1)S(1)} %get-tuple-element.842), channel_id=1, source_target_pairs={{0,32},{32,64},{64,96},{96,128},{128,160},{160,192},{192,224},{224... | collective-permute-start | bytes 294920 | tf_op jit(solution)/shard_map/while/body/eval_jaxpr/ppermute | solution.py:15
  161.6 12.6 %collective-permute-start.1 = (bf16[32,1536]{1,0:T(8,128)(2,1)S(1)}, bf16[32,1536]{1,0:T(8,128)(2,1)S(1)}, u32[]{:S(2)}, u32[]{:S(2)}) collective-permute-start(bf16[32,1536]{1,0:T(8,128)(2,1)S(1)} %get-tuple-element.842), channel_id=1, source_target_pairs={{0,32},{32,64},{64,96},{96,128},{128,160},{160,192},{192,224},{224... | collective-permute-start | bytes 294920 | tf_op jit(solution)/shard_map/while/body/eval_jaxpr/ppermute | solution.py:15
  175.0 7.7 collective-permute-start.1
  183.4 7.7 collective-permute-start.1
  191.8 7.7 collective-permute-start.1
  200.3 8.1 collective-permute-start.1
  209.1 7.8 collective-permute-start.1
  217.6 7.8 collective-permute-start.1
  226.1 7.7 collective-permute-start.1
  234.6 8.6 %collective-permute-start.1 = (bf16[32,1536]{1,0:T(8,128)(2,1)S(1)}, bf16[32,1536]{1,0:T(8,128)(2,1)S(1)}, u32[]{:S(2)}, u32[]{:S(2)}) collective-permute-start(bf16[32,1536]{1,0:T(8,128)(2,1)S(1)} %get-tuple-element.842), channel_id=1, source_target_pairs={{0,32},{32,64},{64,96},{96,128},{128,160},{160,192},{192,224},{224... | collective-permute-start | bytes 294920 | tf_op jit(solution)/shard_map/while/body/eval_jaxpr/ppermute | solution.py:15
  282.2 552.1 %reduce-scatter.2.cloned.1.call-start = ((), (), s32[]{:S(2)}) async-start(), calls=%async_computation.2 | async-start | bytes 835584 | tf_op jit(solution)/shard_map/reduce_scatter | solution.py:153
  452.8 6.7 collective-permute-start
  459.5 6.5 collective-permute-start
  466.0 6.5 collective-permute-start
  472.5 6.5 collective-permute-start
  479.1 7.6 collective-permute-start
  486.6 7.7 collective-permute-start
  494.4 9.0 %collective-permute-start = (bf16[32,1536]{1,0:T(8,128)(2,1)S(1)}, bf16[32,1536]{1,0:T(8,128)(2,1)S(1)}, u32[]{:S(2)}, u32[]{:S(2)}) collective-permute-start(bf16[32,1536]{1,0:T(8,128)(2,1)S(1)} %get-tuple-element.944), channel_id=1, source_target_pairs={{32,0},{64,32},{96,64},{128,96},{160,128},{192,160},{224,192},{256... | collective-permute-start | bytes 294920 | tf_op jit(solution)/shard_map/while/body/eval_jaxpr/ppermute | solution.py:15
  503.4 7.9 collective-permute-start
  511.2 7.6 collective-permute-start
  518.9 7.4 collective-permute-start
  526.3 7.7 collective-permute-start
  534.1 7.7 collective-permute-start
  541.8 7.7 collective-permute-start
  549.6 7.7 collective-permute-start
  557.3 91.9 %collective-permute-start = (bf16[32,1536]{1,0:T(8,128)(2,1)S(1)}, bf16[32,1536]{1,0:T(8,128)(2,1)S(1)}, u32[]{:S(2)}, u32[]{:S(2)}) collective-permute-start(bf16[32,1536]{1,0:T(8,128)(2,1)S(1)} %get-tuple-element.944), channel_id=1, source_target_pairs={{32,0},{64,32},{96,64},{128,96},{160,128},{192,160},{224,192},{256... | collective-permute-start | bytes 294920 | tf_op jit(solution)/shard_map/while/body/eval_jaxpr/ppermute | solution.py:15
  656.5 8.5 %collective-permute-start = (bf16[32,1536]{1,0:T(8,128)(2,1)S(1)}, bf16[32,1536]{1,0:T(8,128)(2,1)S(1)}, u32[]{:S(2)}, u32[]{:S(2)}) collective-permute-start(bf16[32,1536]{1,0:T(8,128)(2,1)S(1)} %get-tuple-element.944), channel_id=1, source_target_pairs={{32,0},{64,32},{96,64},{128,96},{160,128},{192,160},{224,192},{256... | collective-permute-start | bytes 294920 | tf_op jit(solution)/shard_map/while/body/eval_jaxpr/ppermute | solution.py:15
  672.3 8.6 %collective-permute-start = (bf16[32,1536]{1,0:T(8,128)(2,1)S(1)}, bf16[32,1536]{1,0:T(8,128)(2,1)S(1)}, u32[]{:S(2)}, u32[]{:S(2)}) collective-permute-start(bf16[32,1536]{1,0:T(8,128)(2,1)S(1)} %get-tuple-element.944), channel_id=1, source_target_pairs={{32,0},{64,32},{96,64},{128,96},{160,128},{192,160},{224,192},{256... | collective-permute-start | bytes 294920 | tf_op jit(solution)/shard_map/while/body/eval_jaxpr/ppermute | solution.py:15
  688.2 7.5 collective-permute-start
  703.0 7.5 collective-permute-start
  717.9 8.2 collective-permute-start
  733.3 7.7 collective-permute-start
  748.4 8.7 %collective-permute-start = (bf16[32,1536]{1,0:T(8,128)(2,1)S(1)}, bf16[32,1536]{1,0:T(8,128)(2,1)S(1)}, u32[]{:S(2)}, u32[]{:S(2)}) collective-permute-start(bf16[32,1536]{1,0:T(8,128)(2,1)S(1)} %get-tuple-element.944), channel_id=1, source_target_pairs={{32,0},{64,32},{96,64},{128,96},{160,128},{192,160},{224,192},{256... | collective-permute-start | bytes 294920 | tf_op jit(solution)/shard_map/while/body/eval_jaxpr/ppermute | solution.py:15
  764.3 6.6 collective-permute-start
  (3 other events, 372.4 us)
Sparse Core Ops, SparseCore 0:
  282.3 165.5 all-reduce.1
  773.2 61.0 reduce-scatter.1
